TPU v7x, 32 devices: a whole 2x2x4 slice. The times are simulated.
32 devices in a mesh: dp: 8 (over y, x, core), branch: 4 (over z).
Axes of the slice: x: 2, y: 2, z: 4, core: 2. Of those that a mesh axis runs over, the one named last changes fastest.
Arguments:
- tokens: bfloat16 [8192, 2048], P(('dp', 'branch')), may hold values from -6 to 6
- doc_ids: int32 [8192], P('dp'), may hold values from 0 to 15, as said below
- real_rows: int32 [8192], P('dp'), may hold values from 0 to 1, as said below
- cotangent: bfloat16 [8192, 2048], P(('dp', 'branch')), may hold values from -6 to 6
- norm_gain: float32 [2048], P(('dp', 'branch')), may hold values from 0.5 to 1.5
- norm_shift: float32 [2048], P(('dp', 'branch')), may hold values from -2 to 2
- out_bias: float32 [2048], P(('dp', 'branch')), may hold values from -2 to 2
- w_qkv: float32 [3, 2048, 2048], P(None, 'dp', 'branch'), may hold values from -0.125 to 0.125
- b_qkv: float32 [3, 32, 64], P(None, 'branch', 'dp'), may hold values from -3 to 3
- w_out: float32 [2048, 2048], P('branch', 'dp'), may hold values from -0.75 to 0.75
- w_up: float32 [2048, 8192], P('dp', 'branch'), may hold values from -0.125 to 0.125
- b_up: float32 [64, 128], P('branch', 'dp'), may hold values from -3 to 3
- w_down: float32 [8192, 2048], P('branch', 'dp'), may hold values from -0.0625 to 0.0625
Outputs:
- block_out: bfloat16 [8192, 2048], P(('dp', 'branch'))
- tokens_grad: bfloat16 [8192, 2048], P(('dp', 'branch'))
- norm_gain_grad: float32 [2048], P(('dp', 'branch'))
- norm_shift_grad: float32 [2048], P(('dp', 'branch'))
- out_bias_grad: float32 [2048], P(('dp', 'branch'))
- w_qkv_grad: float32 [3, 2048, 2048], P(None, 'dp', 'branch')
- b_qkv_grad: float32 [3, 32, 64], P(None, 'branch', 'dp')
- w_out_grad: float32 [2048, 2048], P('branch', 'dp')
- w_up_grad: float32 [2048, 8192], P('dp', 'branch')
- b_up_grad: float32 [64, 128], P('branch', 'dp')
- w_down_grad: float32 [8192, 2048], P('branch', 'dp')
Inputs may be any that keep to these rules, and one draw needn't show every extreme that they name: `doc_ids`: within each aligned block of 1024 slots the ids start at 0 and never fall; a sequence has 64 times a power of two slots, up to 1024; some sequence has exactly 1024; all padding slots of a block share the id 1024 // 64 - 1, which real slots of a block with padding never take; the last block ends in padding. `real_rows`: within each block, the slots of whole sequences come first and are 1; the rest of the block is 0; every block holds a sequence; the last block ends in padding.
All inputs are finite; a program needn't handle non-finite values.
Results may differ from a plain program's by a relative error of at most 0.014.
Values may be sent and summed in bfloat16 or wider, within the bound.
A program may use at most 192 MiB of HBM per device.

v0:
```python
import math
import jax
import jax.numpy as jnp
from jax import lax
from jax.sharding import PartitionSpec as P

HEAD_DIM = 64
ROT = 32
NORM_EPS = 1e-05
NEGATIVE = -1e30


def positions(doc_rows):
    row_count = doc_rows.shape[0]
    row_index = jnp.arange(row_count, dtype=jnp.int32)
    change = jnp.concatenate([jnp.ones((1,), dtype=bool), doc_rows[1:] != doc_rows[:-1]])
    begins = lax.cummax(jnp.where(change, row_index, jnp.zeros_like(row_index)), axis=0)
    return row_index - begins


def rotary_tables(doc_rows):
    places = positions(doc_rows).astype(jnp.float32)
    half_rot = ROT // 2
    frequency = 10000.0 ** (-2.0 * jnp.arange(half_rot, dtype=jnp.float32) / ROT)
    angles = places[:, None] * frequency[None, :]
    return (jnp.cos(angles), jnp.sin(angles))


def rotate(values, cosine, sine_tab):
    half_rot = ROT // 2
    first_half = values[..., :half_rot]
    second_half = values[..., half_rot : 2 * half_rot]
    remain = values[..., 2 * half_rot :]
    return jnp.concatenate(
        [
            first_half * cosine - second_half * sine_tab,
            second_half * cosine + first_half * sine_tab,
            remain,
        ],
        axis=-1,
    )


def unrotate(values, cosine, sine_tab):
    half_rot = ROT // 2
    first_half = values[..., :half_rot]
    second_half = values[..., half_rot : 2 * half_rot]
    remain = values[..., 2 * half_rot :]
    return jnp.concatenate(
        [
            first_half * cosine + second_half * sine_tab,
            second_half * cosine - first_half * sine_tab,
            remain,
        ],
        axis=-1,
    )


def gelu_tanh(values):
    return jax.nn.gelu(values, approximate=True)


def contract_rows(left, right):
    return lax.dot_general(
        left, right, (((0,), (0,)), ((), ())), preferred_element_type=jnp.float32
    )


def contract_cols(left, right):
    return lax.dot_general(
        left, right, (((1,), (1,)), ((), ())), preferred_element_type=jnp.float32
    )


def masked_scores(query_blk, keys_rot, doc_query, doc_rows, query_index, key_index, factor):
    scores = (
        jnp.einsum("hqd,hkd->hqk", query_blk, keys_rot, preferred_element_type=jnp.float32) * factor
    )
    allowed = (doc_query[:, None] == doc_rows[None, :]) & (
        key_index[None, :] <= query_index[:, None]
    )
    return jnp.where(allowed[None], scores, NEGATIVE)


def local(
    tokens,
    doc_ids,
    real_rows,
    cotangent,
    norm_gain,
    norm_shift,
    out_bias,
    w_qkv,
    b_qkv,
    w_out,
    w_up,
    b_up,
    w_down,
):
    member = lax.axis_index("branch")
    my_rows = tokens.shape[0]
    broadcast_gain, broadcast_shift, bias_full = (
        lax.all_gather(norm_gain.astype(jnp.bfloat16), ("dp", "branch"), axis=0, tiled=True),
        lax.all_gather(norm_shift.astype(jnp.bfloat16), ("dp", "branch"), axis=0, tiled=True),
        lax.all_gather(out_bias.astype(jnp.bfloat16), ("dp", "branch"), axis=0, tiled=True),
    )
    broadcast_gain = broadcast_gain.astype(jnp.float32)
    broadcast_shift = broadcast_shift.astype(jnp.float32)
    bias_full = bias_full.astype(jnp.float32)
    xfloat = tokens.astype(jnp.float32)
    mean_removed = xfloat - jnp.mean(xfloat, axis=-1, keepdims=True)
    inverse_deviation = lax.rsqrt(
        jnp.mean(mean_removed * mean_removed, axis=-1, keepdims=True) + NORM_EPS
    )
    standardized_input = mean_removed * inverse_deviation
    normed_input = (standardized_input * broadcast_gain + broadcast_shift).astype(jnp.bfloat16)
    gathered = lax.all_gather(normed_input, "branch", axis=0, tiled=True)
    row_count = gathered.shape[0]
    attn_w, attn_b, out_w = (
        lax.all_gather(w_qkv.astype(jnp.bfloat16), "dp", axis=1, tiled=True),
        lax.all_gather(b_qkv.astype(jnp.bfloat16), "dp", axis=2, tiled=True),
        lax.all_gather(w_out.astype(jnp.bfloat16), "dp", axis=1, tiled=True),
    )
    up_w, up_b, down_w = (
        lax.all_gather(w_up.astype(jnp.bfloat16), "dp", axis=0, tiled=True),
        lax.all_gather(b_up.astype(jnp.bfloat16), "dp", axis=1, tiled=True),
        lax.all_gather(w_down.astype(jnp.bfloat16), "dp", axis=1, tiled=True),
    )
    local_cols = attn_w.shape[2]
    local_heads = local_cols // HEAD_DIM
    project = jnp.einsum("td,cde->cte", gathered, attn_w, preferred_element_type=jnp.float32)
    project = project + attn_b.astype(jnp.float32).reshape(3, 1, local_cols)
    heads_view = project.reshape(3, row_count, local_heads, HEAD_DIM).transpose(0, 2, 1, 3)
    cosine, sine_tab = rotary_tables(doc_ids)
    queries = rotate(heads_view[0], cosine, sine_tab).astype(jnp.bfloat16)
    keys_rot = rotate(heads_view[1], cosine, sine_tab).astype(jnp.bfloat16)
    values_low = heads_view[2].astype(jnp.bfloat16)
    block_rows = min(512, row_count)
    blocks = row_count // block_rows
    row_index = jnp.arange(row_count, dtype=jnp.int32)
    factor = 1.0 / math.sqrt(HEAD_DIM)
    query_blocks = queries.reshape(local_heads, blocks, block_rows, HEAD_DIM).transpose(1, 0, 2, 3)
    doc_blocks = doc_ids.reshape(blocks, block_rows)
    index_blocks = row_index.reshape(blocks, block_rows)

    def forward_block(pieces):
        query_blk, doc_query, query_index = pieces
        masked = masked_scores(
            query_blk, keys_rot, doc_query, doc_ids, query_index, row_index, factor
        )
        row_top = jnp.max(masked, axis=-1, keepdims=True)
        weights_exp = jnp.exp(masked - row_top)
        row_total = jnp.sum(weights_exp, axis=-1, keepdims=True)
        probability = (weights_exp / row_total).astype(jnp.bfloat16)
        result = jnp.einsum(
            "hqk,hkd->hqd", probability, values_low, preferred_element_type=jnp.float32
        )
        return (result.astype(jnp.bfloat16), (row_top + jnp.log(row_total))[..., 0])

    attended, log_total = lax.map(forward_block, (query_blocks, doc_blocks, index_blocks))
    flat_out = attended.transpose(0, 2, 1, 3).reshape(row_count, local_cols)
    hidden_pre = jnp.dot(gathered, up_w, preferred_element_type=jnp.float32) + up_b.astype(
        jnp.float32
    ).reshape(-1)
    activated = gelu_tanh(hidden_pre).astype(jnp.bfloat16)
    partial_value = jnp.dot(flat_out, out_w, preferred_element_type=jnp.float32)
    partial_value = partial_value + jnp.dot(activated, down_w, preferred_element_type=jnp.float32)
    summed = lax.psum_scatter(
        partial_value.astype(jnp.bfloat16), "branch", scatter_dimension=0, tiled=True
    ).astype(jnp.float32)
    my_real = lax.dynamic_slice_in_dim(real_rows, member * my_rows, my_rows).astype(jnp.float32)
    block_out = (xfloat + my_real[:, None] * (summed + bias_full)).astype(jnp.bfloat16)
    masked_cot = (cotangent.astype(jnp.float32) * my_real[:, None]).astype(jnp.bfloat16)
    cot_all = lax.all_gather(masked_cot, "branch", axis=0, tiled=True)
    bias_part = jnp.sum(masked_cot, axis=0, dtype=jnp.float32)
    down_grad = contract_rows(activated, cot_all)
    hidden_grad = contract_cols(cot_all, down_w)
    gelu_value, gelu_pull = jax.vjp(gelu_tanh, hidden_pre)
    pre_grad = gelu_pull(hidden_grad)[0].astype(jnp.bfloat16)
    up_grad = contract_rows(gathered, pre_grad)
    up_bias_grad = jnp.sum(pre_grad, axis=0, dtype=jnp.float32).reshape(up_b.shape)
    normed_grad = contract_cols(pre_grad, up_w)
    out_grad_w = contract_rows(flat_out, cot_all)
    flat_dout = contract_cols(cot_all, out_w).astype(jnp.bfloat16)
    dout_blocks = flat_dout.reshape(blocks, block_rows, local_heads, HEAD_DIM).transpose(0, 2, 1, 3)

    def backward_block(running_acc, pieces):
        key_acc, value_acc = running_acc
        query_blk, dout_blk, log_blk, doc_query, query_index = pieces
        masked = masked_scores(
            query_blk, keys_rot, doc_query, doc_ids, query_index, row_index, factor
        )
        probability = jnp.exp(masked - log_blk[..., None])
        value_acc = value_acc + jnp.einsum(
            "hqk,hqd->hkd",
            probability.astype(jnp.bfloat16),
            dout_blk,
            preferred_element_type=jnp.float32,
        )
        prob_grad = jnp.einsum(
            "hqd,hkd->hqk", dout_blk, values_low, preferred_element_type=jnp.float32
        )
        score_grad = probability * (
            prob_grad - jnp.sum(probability * prob_grad, axis=-1, keepdims=True)
        )
        score_grad = score_grad.astype(jnp.bfloat16)
        query_grad = (
            jnp.einsum("hqk,hkd->hqd", score_grad, keys_rot, preferred_element_type=jnp.float32)
            * factor
        )
        key_acc = (
            key_acc
            + jnp.einsum("hqk,hqd->hkd", score_grad, query_blk, preferred_element_type=jnp.float32)
            * factor
        )
        return ((key_acc, value_acc), query_grad)

    zero_acc = jnp.zeros((local_heads, row_count, HEAD_DIM), jnp.float32)
    (key_grad, value_grad), query_grads = lax.scan(
        backward_block,
        (zero_acc, zero_acc),
        (query_blocks, dout_blocks, log_total, doc_blocks, index_blocks),
    )
    query_grad = query_grads.transpose(1, 0, 2, 3).reshape(local_heads, row_count, HEAD_DIM)
    stacked = jnp.stack(
        [unrotate(query_grad, cosine, sine_tab), unrotate(key_grad, cosine, sine_tab), value_grad]
    )
    qkv_grad = stacked.transpose(0, 2, 1, 3).reshape(3, row_count, local_cols).astype(jnp.bfloat16)
    attn_grad_w = jnp.einsum("td,cte->cde", gathered, qkv_grad, preferred_element_type=jnp.float32)
    attn_bias_grad = jnp.sum(qkv_grad, axis=1, dtype=jnp.float32).reshape(attn_b.shape)
    normed_grad = normed_grad + jnp.einsum(
        "cte,cde->td", qkv_grad, attn_w, preferred_element_type=jnp.float32
    )
    w_qkv_grad, b_qkv_grad, w_out_grad, w_up_grad, b_up_grad, w_down_grad = (
        lax.psum_scatter(
            attn_grad_w.astype(jnp.bfloat16), "dp", scatter_dimension=1, tiled=True
        ).astype(jnp.float32),
        lax.psum_scatter(
            attn_bias_grad.astype(jnp.bfloat16), "dp", scatter_dimension=2, tiled=True
        ).astype(jnp.float32),
        lax.psum_scatter(
            out_grad_w.astype(jnp.bfloat16), "dp", scatter_dimension=1, tiled=True
        ).astype(jnp.float32),
        lax.psum_scatter(
            up_grad.astype(jnp.bfloat16), "dp", scatter_dimension=0, tiled=True
        ).astype(jnp.float32),
        lax.psum_scatter(
            up_bias_grad.astype(jnp.bfloat16), "dp", scatter_dimension=1, tiled=True
        ).astype(jnp.float32),
        lax.psum_scatter(
            down_grad.astype(jnp.bfloat16), "dp", scatter_dimension=1, tiled=True
        ).astype(jnp.float32),
    )
    normed_total_sum = lax.psum_scatter(
        normed_grad.astype(jnp.bfloat16), "branch", scatter_dimension=0, tiled=True
    ).astype(jnp.float32)
    scaled_input = normed_total_sum * broadcast_gain
    input_grad = inverse_deviation * (
        scaled_input
        - jnp.mean(scaled_input, axis=-1, keepdims=True)
        - standardized_input * jnp.mean(scaled_input * standardized_input, axis=-1, keepdims=True)
    )
    tokens_grad = (cotangent.astype(jnp.float32) + input_grad).astype(jnp.bfloat16)
    gain_sums, shift_sums, bias_sums = (
        lax.psum_scatter(
            jnp.sum(normed_total_sum * standardized_input, axis=0),
            ("dp", "branch"),
            scatter_dimension=0,
            tiled=True,
        ),
        lax.psum_scatter(
            jnp.sum(normed_total_sum, axis=0), ("dp", "branch"), scatter_dimension=0, tiled=True
        ),
        lax.psum_scatter(bias_part, ("dp", "branch"), scatter_dimension=0, tiled=True),
    )
    return (
        block_out,
        tokens_grad,
        gain_sums,
        shift_sums,
        bias_sums,
        w_qkv_grad,
        b_qkv_grad,
        w_out_grad,
        w_up_grad,
        b_up_grad,
        w_down_grad,
    )


def solution(mesh):
    in_specs = (
        P(("dp", "branch"), None),
        P("dp"),
        P("dp"),
        P(("dp", "branch"), None),
        P(("dp", "branch")),
        P(("dp", "branch")),
        P(("dp", "branch")),
        P(None, "dp", "branch"),
        P(None, "branch", "dp"),
        P("branch", "dp"),
        P("dp", "branch"),
        P("branch", "dp"),
        P("branch", "dp"),
    )
    out_specs = (
        P(("dp", "branch"), None),
        P(("dp", "branch"), None),
        P(("dp", "branch")),
        P(("dp", "branch")),
        P(("dp", "branch")),
        P(None, "dp", "branch"),
        P(None, "branch", "dp"),
        P("branch", "dp"),
        P("dp", "branch"),
        P("branch", "dp"),
        P("branch", "dp"),
    )
    return jax.shard_map(local, mesh=mesh, in_specs=in_specs, out_specs=out_specs, check_vma=False)
```

profile of v0, /device:TPU:0, one launch (start us, length us, event | category | flops | bytes accessed | tf_op | source)
XLA Modules:
  0.0 864.9 jit_solution(15730923838003511770)
XLA Ops:
  10.5 3.1 convert_reduce_fusion.2
  14.5 42.2 %all-reduce.8 = (bf16[2048]{0:T(1024)(128)(2,1)S(1)}, bf16[2048]{0:T(1024)(128)(2,1)S(1)}, bf16[2048]{0:T(1024)(128)(2,1)}) all-reduce(bf16[2048]{0:T(1024)(128)(2,1)S(1)} %dynamic-update-slice.1, bf16[2048]{0:T(1024)(128)(2,1)S(1)} %dynamic-update-slice, ...), channel_id=1, replica_groups=mesh['dp'=8,'branch'=4] {'dp','branch'}, use_global_device_ids=true, to_apply=%add.1 | all-reduce | flops 6144 | bytes 24576
  66.5 10.4 %all_gather.37 = bf16[3,8,64]{1,0,2:T(4,128)(2,1)S(1)} all-gather(bf16[3,8,8]{1,0,2:T(4,128)(2,1)S(1)} %copy.73), channel_id=1, replica_groups=mesh['dp'=8,'branch'=4] {'dp'}, dimensions={2}, use_global_device_ids=true | all-gather | bytes 3456 | tf_op jit(solution)/shard_map/all_gather | solution.py:121
  77.8 8.1 all_gather.40
  87.0 37.6 %all-gather.17.cloned.1.call-done = bf16[1024,2048]{1,0:T(8,128)(2,1)} async-done(((bf16[256,2048]{1,0:T(8,128)(2,1)}), bf16[1024,2048]{1,0:T(8,128)(2,1)}) %all-gather.17.cloned.1.call-update) | async-done | bytes 4194320 | tf_op jit(solution)/shard_map/all_gather | solution.py:174
  124.6 5.2 convolution_convert_fusion.3
  132.8 73.2 %all-gather.7.cloned.1.call-done = bf16[1024,2048]{1,0:T(8,128)(2,1)} async-done(((bf16[256,2048]{1,0:T(8,128)(2,1)}), bf16[1024,2048]{1,0:T(8,128)(2,1)}) %all-gather.7.cloned.1.call-update) | async-done | bytes 4194320 | tf_op jit(solution)/shard_map/all_gather | solution.py:117
  206.0 47.0 %all-gather.9.cloned.1.call-done = bf16[3,2048,512]{1,2,0:T(8,128)(2,1)} async-done(((bf16[3,256,512]{1,2,0:T(8,128)(2,1)}), bf16[3,2048,512]{1,2,0:T(8,128)(2,1)}) %all-gather.9.cloned.1.call-update) | async-done | bytes 6291472 | tf_op jit(solution)/shard_map/all_gather | solution.py:120
  253.0 10.1 %broadcast_add_fusion = f32[1024,3,512]{0,2,1:T(8,128)S(1)} fusion(f32[3,512]{1,0:T(4,128)S(1)} %reshape.336, bf16[3,2048,512]{1,2,0:T(8,128)(2,1)} %all-gather.9.cloned.1.call-done, bf16[1024,2048]{1,0:T(8,128)(2,1)} %all-gather.7.cloned.1.call-done), kind=kOutput, calls=%fused_computation.73 | convolution fusion | flops 6444023808 | bytes 16783360 | tf_op jit(solution)/shard_map/td,cde->cte/dot_general | solution.py:131
  266.6 31.2 %while.28 = (s32[]{:T(128)}, bf16[2,8,512,64]{2,3,1,0:T(8,128)(2,1)S(1)}, f32[2,8,512]{2,1,0:T(8,128)}, s32[2,512]{1,0:T(2,128)S(1)}, s32[1024]{0:T(1024)S(1)}, ...) while((s32[]{:T(128)}, ...), condition=%wide.region_7.8_spmd.clone, body=%wide.region_4.7_spmd.clone.sunk | while | flops 1125904384 | bytes 55723116 | solution.py:160
  267.2 4.1 fusion.124
  271.3 4.2 fusion.125
  276.2 5.9 fusion.126
  282.7 4.3 fusion.124
  287.0 4.2 fusion.125
  291.9 5.9 fusion.126
  298.7 96.8 %while.29 = (s32[]{:T(128)}, f32[8,1024,64]{1,2,0:T(8,128)}, f32[8,1024,64]{1,2,0:T(8,128)}, f32[2,8,512,64]{2,3,1,0:T(8,128)}, s32[2,512]{1,0:T(2,128)S(1)}, /*...) while((s32[]{:T(128)}, f32[8,1024,64]{1,2,0:T(8,128)}, ...), condition=%wide.region_11.12_spmd.clone, body=%wide.region_9.11_spmd.clone.sunk | while | flops 2726555648 | bytes 229869888 | solution.py:219
  300.3 3.8 fusion.136
  304.7 11.4 %multiply_reduce_fusion.2 = (f32[8,512]{1,0:T(8,128)}, f32[8,512,1024]{2,1,0:T(8,128)}) fusion(f32[8,512,1024]{2,1,0:T(8,128)S(1)} %fusion.136, f32[8,512]{1,0:T(8,128)} %dynamic-slice_bitcast_fusion.2, bf16[8,1024,64]{1,2,0:T(8,128)(2,1)S(1)} %get-tuple-element.598, bf16[2,8,512,64]{2,3,1,0:T(8,128)(2,1)} %get-tuple-element.597, ...), kind=kOutput, calls=%fused_computation.23.clone.1 | convolution fusion | flops 557838336 | bytes 35684864 | tf_op jit(solution)/shard_map/while/body/eval_jaxpr/hqd,hkd->hqk/dot_general | solution.py:77
  316.1 10.9 %multiply_convert_fusion.5 = bf16[8,512,1024]{2,1,0:T(8,128)(2,1)} fusion(f32[8,512,1024]{2,1,0:T(8,128)} %get-tuple-element.530, f32[8,512,1024]{2,1,0:T(8,128)S(1)} %fusion.136, f32[8,512]{1,0:T(8,128)} %get-tuple-element.531), kind=kLoop, calls=%fused_computation.22.clone.1 | loop fusion | flops 12582912 | bytes 41959424 | tf_op jit(solution)/shard_map/while/body/eval_jaxpr/convert_element_type | solution.py:206
  327.0 7.2 fusion.138
  334.2 5.5 select_add_fusion.4
  339.7 4.6 copy-done
  344.6 2.9 select_add_fusion.5
  348.8 3.8 fusion.136
  353.2 11.5 %multiply_reduce_fusion.2 = (f32[8,512]{1,0:T(8,128)}, f32[8,512,1024]{2,1,0:T(8,128)}) fusion(f32[8,512,1024]{2,1,0:T(8,128)S(1)} %fusion.136, f32[8,512]{1,0:T(8,128)} %dynamic-slice_bitcast_fusion.2, bf16[8,1024,64]{1,2,0:T(8,128)(2,1)S(1)} %get-tuple-element.598, bf16[2,8,512,64]{2,3,1,0:T(8,128)(2,1)} %get-tuple-element.597, ...), kind=kOutput, calls=%fused_computation.23.clone.1 | convolution fusion | flops 557838336 | bytes 35684864 | tf_op jit(solution)/shard_map/while/body/eval_jaxpr/hqd,hkd->hqk/dot_general | solution.py:77
  364.7 9.5 %multiply_convert_fusion.5 = bf16[8,512,1024]{2,1,0:T(8,128)(2,1)} fusion(f32[8,512,1024]{2,1,0:T(8,128)} %get-tuple-element.530, f32[8,512,1024]{2,1,0:T(8,128)S(1)} %fusion.136, f32[8,512]{1,0:T(8,128)} %get-tuple-element.531), kind=kLoop, calls=%fused_computation.22.clone.1 | loop fusion | flops 12582912 | bytes 41959424 | tf_op jit(solution)/shard_map/while/body/eval_jaxpr/convert_element_type | solution.py:206
  374.3 7.3 fusion.138
  381.5 5.5 select_add_fusion.4
  387.0 3.6 copy-done
  390.8 4.5 select_add_fusion.5
  400.3 3.7 convolution_convert_fusion.2
  406.7 14.7 %fusion.74 = f32[1024,2048]{1,0:T(8,128)} fusion(bf16[1024,2048]{1,0:T(8,128)(2,1)} %all-gather.7.cloned.1.call-done, bf16[2048,2048]{1,0:T(8,128)(2,1)} %all-gather.13.cloned.1.call-done), kind=kOutput, calls=%fused_computation.140 | convolution fusion | flops 8589934592 | bytes 20971520 | tf_op jit(solution)/shard_map/dot_general | solution.py:162
  421.4 20.3 %fusion.70 = (bf16[2048]{0:T(1024)(128)(2,1)S(1)}, bf16[1024,2048]{1,0:T(8,128)(2,1)}) fusion(f32[1024,2048]{1,0:T(8,128)} %fusion.74, f32[2048]{0:T(1024)S(1)} %copy-done.32, bf16[1024,2048]{1,0:T(8,128)(2,1)} %all-gather.17.cloned.1.call-done, bf16[2048,2048]{1,0:T(8,128)(2,1)} %all-gather.15.cloned.1.call-done), kind=kOutput, calls=%fused_computation.138 | convolution fusion | flops 8636069888 | bytes 25178112 | tf_op jit(solution)/shard_map/dot_general | solution.py:70
  442.5 11.2 %convert_bitcast_fusion = bf16[3,2048,512]{1,2,0:T(8,128)(2,1)} fusion(bf16[3,1024,512]{1,2,0:T(8,128)(2,1)S(1)} %bitcast.179, bf16[1024,2048]{1,0:T(8,128)(2,1)} %all-gather.7.cloned.1.call-done), kind=kOutput, calls=%fused_computation.66 | convolution fusion | flops 6445596672 | bytes 13631488 | tf_op jit(solution)/shard_map/td,cte->cde/dot_general | solution.py:229
  453.8 12.6 %fusion.75 = f32[1024,2048]{1,0:T(8,128)S(1)} fusion(bf16[1024,2048]{1,0:T(8,128)(2,1)} %get-tuple-element.355, bf16[2048,2048]{1,0:T(8,128)(2,1)} %all-gather.13.cloned.1.call-done), kind=kOutput, calls=%fused_computation.141 | convolution fusion | flops 8589934592 | bytes 20971520 | tf_op jit(solution)/shard_map/dot_general | solution.py:70
  466.4 11.2 %fusion.44 = bf16[1024,2048]{1,0:T(8,128)(2,1)} fusion(f32[1024,2048]{1,0:T(8,128)S(1)} %fusion.75, bf16[3,1024,512]{1,2,0:T(8,128)(2,1)S(1)} %bitcast.180, bf16[3,2048,512]{1,2,0:T(8,128)(2,1)} %all-gather.9.cloned.1.call-done), kind=kOutput, calls=%fused_computation.60 | convolution fusion | flops 6446645248 | bytes 22020096 | tf_op jit(solution)/shard_map/cte,cde->td/dot_general | solution.py:231
  477.7 15.8 %fusion.69 = f32[1024,2048]{1,0:T(8,128)S(1)} fusion(bf16[2048,2048]{1,0:T(8,128)(2,1)} %all-gather.15.cloned.1.call-done, f32[1024,2048]{1,0:T(8,128)} %fusion.74, f32[2048]{0:T(1024)S(1)} %copy-done.32), kind=kOutput, calls=%fused_computation.137 | convolution fusion | flops 8610906112 | bytes 25174016 | tf_op jit(solution)/shard_map/dot_general | solution.py:167
  493.5 4.3 add_convert_fusion
  497.9 14.2 %convolution_convert_fusion.1 = bf16[2048,2048]{1,0:T(8,128)(2,1)} fusion(bf16[1024,2048]{1,0:T(8,128)(2,1)} %all-gather.7.cloned.1.call-done, bf16[1024,2048]{1,0:T(8,128)(2,1)} %get-tuple-element.355), kind=kOutput, calls=%fused_computation.64 | convolution fusion | flops 8594128896 | bytes 16777216 | tf_op jit(solution)/shard_map/dot_general | solution.py:64
  512.2 16.2 %convolution_convert_fusion = bf16[2048,2048]{1,0:T(8,128)(2,1)} fusion(bf16[1024,2048]{1,0:T(8,128)(2,1)} %all-gather.17.cloned.1.call-done, f32[1024,2048]{1,0:T(8,128)} %fusion.74, f32[2048]{0:T(1024)S(1)} %copy-done.32), kind=kOutput, calls=%fused_computation.63 | convolution fusion | flops 8615100416 | bytes 20979712 | tf_op jit(solution)/shard_map/dot_general | solution.py:64
  530.3 12.9 %all-reduce.6 = bf16[3,8,64]{2,1,0:T(8,128)(2,1)S(1)} all-reduce(bf16[3,8,64]{2,1,0:T(8,128)(2,1)S(1)} %copy-done.25), channel_id=8, replica_groups=mesh['dp'=8,'branch'=4] {'dp'}, use_global_device_ids=true, to_apply=%region_23.24.clone | all-reduce | flops 1536 | bytes 6144
  549.6 74.9 %reduce-scatter.13.cloned.1.call-done = bf16[256,2048]{1,0:T(8,128)(2,1)} async-done(((bf16[1024,2048]{1,0:T(8,128)(2,1)}), bf16[256,2048]{1,0:T(8,128)(2,1)}) %reduce-scatter.13.cloned.1.call-update) | async-done | bytes 1048592 | tf_op jit(solution)/shard_map/reduce_scatter | solution.py:254
  626.8 46.3 %all-reduce.7 = (f32[2048]{0:T(1024)S(1)}, f32[2048]{0:T(1024)S(1)}, f32[2048]{0:T(1024)S(1)}) all-reduce(f32[2048]{0:T(1024)S(1)} %get-tuple-element.302, f32[2048]{0:T(1024)S(1)} %get-tuple-element.305, f32[2048]{0:T(1024)S(1)} %copy-done.22), channel_id=4, replica_groups=mesh['dp'=8,'branch'=4] {'dp','branch'}, use_global_device_ids=true, to_apply=%region_16.17.clone | all-reduce | flops 6144 | bytes 49152
  674.8 30.3 %reduce-scatter.11.cloned.1.call-done = bf16[256,2048]{1,0:T(8,128)(2,1)} async-done(((bf16[1024,2048]{1,0:T(8,128)(2,1)}), bf16[256,2048]{1,0:T(8,128)(2,1)}) %reduce-scatter.11.cloned.1.call-update) | async-done | bytes 1048592 | tf_op jit(solution)/shard_map/reduce_scatter | solution.py:168
  705.1 4.0 fusion.63
  709.1 71.5 %reduce-scatter.19.cloned.1.call-done = bf16[256,2048]{1,0:T(8,128)(2,1)} async-done(((bf16[2048,2048]{1,0:T(8,128)(2,1)}), bf16[256,2048]{1,0:T(8,128)(2,1)}) %reduce-scatter.19.cloned.1.call-update) | async-done | bytes 1048592 | tf_op jit(solution)/shard_map/reduce_scatter | solution.py:244
  783.5 72.0 %reduce-scatter.21.cloned.1.call-done = bf16[2048,256]{1,0:T(8,128)(2,1)} async-done(((bf16[2048,2048]{1,0:T(8,128)(2,1)}), bf16[2048,256]{1,0:T(8,128)(2,1)}) %reduce-scatter.21.cloned.1.call-update) | async-done | bytes 1048592 | tf_op jit(solution)/shard_map/reduce_scatter | solution.py:250
  (213 shorter events, 55.5 us)
Async XLA Ops:
  7.2 6.5 copy-start.36
  7.2 6.5 copy-start.37
  7.2 6.5 copy-start.38
  7.2 49.4 %copy-start.5 = (bf16[256,2048]{1,0:T(8,128)(2,1)S(1)}, bf16[256,2048]{1,0:T(8,128)(2,1)}, u32[]{:S(2)}) copy-start(bf16[256,2048]{1,0:T(8,128)(2,1)} %param.17) | copy-start | bytes 3145732
  7.2 79.7 %all-gather.11.cloned.1.call-start = ((), (), s32[]{:S(2)}) async-start(), calls=%async_computation.9 | async-start | bytes 2359296 | tf_op jit(solution)/shard_map/all_gather | solution.py:122
  9.1 115.4 %all-gather.17.cloned.1.call-start = ((), (), s32[]{:S(2)}) async-start(), calls=%async_computation.13 | async-start | bytes 5242880 | tf_op jit(solution)/shard_map/all_gather | solution.py:174
  13.6 192.4 %all-gather.7.cloned.1.call-start = ((), (), s32[]{:S(2)}) async-start(), calls=%async_computation.7 | async-start | bytes 5242880 | tf_op jit(solution)/shard_map/all_gather | solution.py:117
  56.7 5.6 copy-start.8
  59.5 193.5 %all-gather.9.cloned.1.call-start = ((), (), s32[]{:S(2)}) async-start(), calls=%async_computation.8 | async-start | bytes 7077888 | tf_op jit(solution)/shard_map/all_gather | solution.py:120
  62.2 4.1 copy-start.14
  62.2 4.2 copy-start.28
  62.2 15.5 %copy-start.31 = (f32[16,16]{1,0:T(8,128)S(1)}, f32[16,16]{1,0:T(8,128)}, u32[]{:S(2)}) copy-start(f32[16,16]{1,0:T(8,128)} %param.28) | copy-start | bytes 3076
  62.3 344.5 %all-gather.13.cloned.1.call-start = ((), (), s32[]{:S(2)}) async-start(), calls=%async_computation.10 | async-start | bytes 9437184 | tf_op jit(solution)/shard_map/all_gather | solution.py:125
  63.5 358.0 %all-gather.15.cloned.1.call-start = ((), (), s32[]{:S(2)}) async-start(), calls=%async_computation.11 | async-start | bytes 9437184 | tf_op jit(solution)/shard_map/all_gather | solution.py:127
  66.2 477.7 %reduce-scatter.17.cloned.1.call-start = ((), (), s32[]{:S(2)}) async-start(), calls=%async_computation.16 | async-start | bytes 2359296 | tf_op jit(solution)/shard_map/reduce_scatter | solution.py:241
  86.9 178.1 %copy-start.15 = (f32[1024,16]{0,1:T(8,128)}, f32[1024,16]{0,1:T(8,128)S(1)}, u32[]{:S(2)}) copy-start(f32[1024,16]{0,1:T(8,128)S(1)} %get-tuple-element.384) | copy-start | bytes 196612
  86.9 178.1 %copy-start.17 = (f32[1024,16]{0,1:T(8,128)}, f32[1024,16]{0,1:T(8,128)S(1)}, u32[]{:S(2)}) copy-start(f32[1024,16]{0,1:T(8,128)S(1)} %get-tuple-element.385) | copy-start | bytes 196612
  300.3 3.8 copy-start.19
  327.0 7.2 copy-start.1
  334.2 10.0 %copy-start = (f32[8,512,1024]{2,1,0:T(8,128)S(1)}, f32[8,512,1024]{2,1,0:T(8,128)}, u32[]{:S(2)}) copy-start(f32[8,512,1024]{2,1,0:T(8,128)} %get-tuple-element.530) | copy-start | bytes 50331652 | tf_op jit(solution)/shard_map/while
  334.2 10.3 %copy-start.4 = (bf16[2,8,512,64]{2,3,1,0:T(8,128)(2,1)S(1)}, bf16[2,8,512,64]{2,3,1,0:T(8,128)(2,1)}, u32[]{:S(2)}) copy-start(bf16[2,8,512,64]{2,3,1,0:T(8,128)(2,1)} %get-tuple-element.600) | copy-start | bytes 3145732 | tf_op jit(solution)/shard_map/while
  339.7 7.7 copy-start.2
  348.8 3.8 copy-start.19
  374.3 7.3 copy-start.1
  381.5 9.1 %copy-start = (f32[8,512,1024]{2,1,0:T(8,128)S(1)}, f32[8,512,1024]{2,1,0:T(8,128)}, u32[]{:S(2)}) copy-start(f32[8,512,1024]{2,1,0:T(8,128)} %get-tuple-element.530) | copy-start | bytes 50331652 | tf_op jit(solution)/shard_map/while
  381.5 9.3 %copy-start.4 = (bf16[2,8,512,64]{2,3,1,0:T(8,128)(2,1)S(1)}, bf16[2,8,512,64]{2,3,1,0:T(8,128)(2,1)}, u32[]{:S(2)}) copy-start(bf16[2,8,512,64]{2,3,1,0:T(8,128)(2,1)} %get-tuple-element.600) | copy-start | bytes 3145732 | tf_op jit(solution)/shard_map/while
  387.0 8.3 copy-start.2
  395.5 2.2 copy-start.3
  395.5 2.5 copy-start.11
  397.5 1.9 copy-start.16
  397.8 2.6 copy-start.34
  404.1 141.6 %reduce-scatter.23.cloned.1.call-start = ((), (), s32[]{:S(2)}) async-start(), calls=%async_computation.19 | async-start | bytes 36864
  406.7 14.7 %copy-start.32 = (f32[2048]{0:T(1024)S(1)}, f32[2048]{0:T(1024)}, u32[]{:S(2)}) copy-start(f32[2048]{0:T(1024)} %bitcast_convert_fusion) | copy-start | bytes 24580
  442.5 104.5 %reduce-scatter.15.cloned.1.call-start = ((), (), s32[]{:S(2)}) async-start(), calls=%async_computation.15 | async-start | bytes 7077888 | tf_op jit(solution)/shard_map/reduce_scatter | solution.py:235
  453.7 170.7 %reduce-scatter.13.cloned.1.call-start = ((), (), s32[]{:S(2)}) async-start(), calls=%async_computation.14 | async-start | bytes 5242880 | tf_op jit(solution)/shard_map/reduce_scatter | solution.py:254
  477.6 15.9 %copy-start.13 = (bf16[64,8,2,512]{3,1,2,0:T(8,128)(2,1)S(1)}, bf16[64,8,2,512]{3,1,2,0:T(8,128)(2,1)}, u32[]{:S(2)}) copy-start(bf16[64,8,2,512]{3,1,2,0:T(8,128)(2,1)} %copy-done.12) | copy-start | bytes 3145732
  477.6 15.9 %copy-start.35 = (bf16[512,2048]{1,0:T(8,128)(2,1)S(1)}, bf16[512,2048]{1,0:T(8,128)(2,1)}, u32[]{:S(2)}) copy-start(bf16[512,2048]{1,0:T(8,128)(2,1)} %all-gather.11.cloned.1.call-done) | copy-start | bytes 6291460
  477.6 227.5 %reduce-scatter.11.cloned.1.call-start = ((), (), s32[]{:S(2)}) async-start(), calls=%async_computation.12 | async-start | bytes 5242880 | tf_op jit(solution)/shard_map/reduce_scatter | solution.py:168
  497.9 282.8 %reduce-scatter.19.cloned.1.call-start = ((), (), s32[]{:S(2)}) async-start(), calls=%async_computation.17 | async-start | bytes 9437184 | tf_op jit(solution)/shard_map/reduce_scatter | solution.py:244
  512.1 343.3 %reduce-scatter.21.cloned.1.call-start = ((), (), s32[]{:S(2)}) async-start(), calls=%async_computation.18 | async-start | bytes 9437184 | tf_op jit(solution)/shard_map/reduce_scatter | solution.py:250
  528.4 1.9 copy-start.25
  528.4 96.1 %copy-start.6 = (bf16[256,2048]{1,0:T(8,128)(2,1)S(1)}, bf16[256,2048]{1,0:T(8,128)(2,1)}, u32[]{:S(2)}) copy-start(bf16[256,2048]{1,0:T(8,128)(2,1)} %param.17) | copy-start | bytes 3145732
  528.4 96.1 %copy-start.21 = (f32[2048]{0:T(1024)S(1)}, f32[2048]{0:T(1024)}, u32[]{:S(2)}) copy-start(f32[2048]{0:T(1024)} %copy-done.20) | copy-start | bytes 24580
  528.4 96.0 %copy-start.24 = (f32[256]{0:T(256)S(1)}, f32[256]{0:T(256)}, u32[]{:S(2)}) copy-start(f32[256]{0:T(256)} %copy-done.23) | copy-start | bytes 3076
  528.4 96.0 %copy-start.27 = (f32[256]{0:T(256)S(1)}, f32[256]{0:T(256)}, u32[]{:S(2)}) copy-start(f32[256]{0:T(256)} %copy-done.26) | copy-start | bytes 3076
  528.5 98.3 %copy-start.22 = (f32[2048]{0:T(1024)S(1)}, f32[2048]{0:T(1024)}, u32[]{:S(2)}) copy-start(f32[2048]{0:T(1024)} %get-tuple-element.358) | copy-start | bytes 24580
  528.5 176.6 %copy-start.7 = (bf16[256,2048]{1,0:T(8,128)(2,1)S(1)}, bf16[256,2048]{1,0:T(8,128)(2,1)}, u32[]{:S(2)}) copy-start(bf16[256,2048]{1,0:T(8,128)(2,1)} %param.20) | copy-start | bytes 3145732
  528.5 176.6 %copy-start.30 = (f32[256]{0:T(256)S(1)}, f32[256]{0:T(256)}, u32[]{:S(2)}) copy-start(f32[256]{0:T(256)} %copy-done.29) | copy-start | bytes 3076
  (10 other events, 9.1 us)
Sparse Core Ops, SparseCore 0:
  10.5 31.0 all-gather.10
  43.8 80.7 all-gather.16
  126.7 79.2 all-gather.6
  207.8 45.1 all-gather.8
  255.3 54.4 all-gather.12
  311.5 55.9 all-gather.14
  404.2 40.4 reduce-scatter.16
  448.5 31.2 reduce-scatter.22
  483.2 62.1 reduce-scatter.14
  547.6 76.8 reduce-scatter.12
  626.8 78.2 reduce-scatter.10
  708.8 71.8 reduce-scatter.18
  784.1 71.2 reduce-scatter.20
where the time goes:
time: 872 us; the launch traced here: 865 us
  waiting for transfers between devices  407 us (47%)
  matrix products  223 us (26%)
  blocking collectives  120 us (14%)
  other arithmetic  66.4 us (8%)
  local copies, waits for them, and re-layouts  32.5 us (4%)
  between operations  15.5 us (2%)
    unnamed x3, blocking collectives  101 us
    reduce_scatter x1, waiting for transfers between devices, local(): lax.psum_scatter(normed_grad.astype(jnp.bfloat16), 'branch', scatter_dime...  74.9 us
    all_gather x1, waiting for transfers between devices, local(): gathered = lax.all_gather(normed_input, 'branch', axis=0, tiled=True)  73.2 us
    reduce_scatter x1, waiting for transfers between devices, local(): lax.psum_scatter(down_grad.astype(jnp.bfloat16), 'dp', scatter_dimension=...  72 us
    reduce_scatter x1, waiting for transfers between devices, local(): lax.psum_scatter(up_grad.astype(jnp.bfloat16), 'dp', scatter_dimension=0,...  71.5 us
    all_gather x1, waiting for transfers between devices, local(): lax.all_gather(w_qkv.astype(jnp.bfloat16), 'dp', axis=1, tiled=True)  47 us
    dot_general x3, matrix products, contract_cols(): lax.dot_general(left, right, (((1,), (1,)), ((), ())), preferred_element_...  38.1 us
    all_gather x1, waiting for transfers between devices, local(): cot_all = lax.all_gather(masked_cot, 'branch', axis=0, tiled=True)  37.6 us
  transfers between devices with their start and end apart: 13, of which 7 were waited for; matrix products, arithmetic and copies ran while one was open for 35% of the time, Pallas kernels for 0%

commit v1 on v0

--- a/solution.py
+++ b/solution.py
@@ -171,7 +171,13 @@
     my_real = lax.dynamic_slice_in_dim(real_rows, member * my_rows, my_rows).astype(jnp.float32)
     block_out = (xfloat + my_real[:, None] * (summed + bias_full)).astype(jnp.bfloat16)
     masked_cot = (cotangent.astype(jnp.float32) * my_real[:, None]).astype(jnp.bfloat16)
-    cot_all = lax.all_gather(masked_cot, "branch", axis=0, tiled=True)
+    size = lax.axis_size("branch")
+    held, parts = (masked_cot, [masked_cot])
+    for _ in range(size - 1):
+        held = lax.ppermute(held, "branch", [(i, (i + 1) % size) for i in range(size)])
+        parts.insert(0, held)
+    line = jnp.concatenate(parts, axis=0)
+    cot_all = jnp.roll(line, (lax.axis_index("branch") + 1) * masked_cot.shape[0], axis=0)
     bias_part = jnp.sum(masked_cot, axis=0, dtype=jnp.float32)
     down_grad = contract_rows(activated, cot_all)
     hidden_grad = contract_cols(cot_all, down_w)

time: 872 us -> 856 us (0.982)
  waiting for transfers between devices: 407 us -> 342 us
  starting transfers between devices: 0.54 us -> 26.6 us
  local copies, waits for them, and re-layouts: 32.5 us -> 44.8 us
    ppermute x0 -> x3, waiting for transfers between devices: none -> 90.4 us  [local(): lax.ppermute(held, 'branch', [(i, (i + 1) % size) for i in range(size)])]
    all_gather x1, waiting for transfers between devices: 73.2 us -> 0.01 us  [local(): gathered = lax.all_gather(normed_input, 'branch', axis=0, tiled=True)]
    all_gather x1, waiting for transfers between devices: 47 us -> 5.43 us  [local(): lax.all_gather(w_qkv.astype(jnp.bfloat16), 'dp', axis=1, tiled=True)]
    all_gather x1 -> x0, waiting for transfers between devices: 37.6 us -> none  [local(): cot_all = lax.all_gather(masked_cot, 'branch', axis=0, tiled=True)]
    ppermute x0 -> x3, starting transfers between devices: none -> 26.1 us  [local(): lax.ppermute(held, 'branch', [(i, (i + 1) % size) for i in range(size)])]
    unnamed x87 -> x80, local copies, waits for them, and re-layouts: 15.2 us -> 23.4 us
  transfers between devices with their start and end apart: 13 -> 15, of which waited for: 7 -> 8; matrix products, arithmetic and copies ran while one was open for 35% -> 39% of each run, Pallas kernels for 0% -> 0%
where the time goes in v1:
time: 856 us; the launch traced here: 848 us
  waiting for transfers between devices  342 us (40%)
  matrix products  228 us (27%)
  blocking collectives  121 us (14%)
  other arithmetic  70.2 us (8%)
  local copies, waits for them, and re-layouts  44.8 us (5%)
  starting transfers between devices  26.6 us (3%)
  between operations  15.7 us (2%)
    unnamed x3, blocking collectives  103 us
    ppermute x3, waiting for transfers between devices, local(): lax.ppermute(held, 'branch', [(i, (i + 1) % size) for i in range(size)])  90.4 us
    reduce_scatter x1, waiting for transfers between devices, local(): lax.psum_scatter(up_grad.astype(jnp.bfloat16), 'dp', scatter_dimension=0,...  72 us
    reduce_scatter x1, waiting for transfers between devices, local(): lax.psum_scatter(down_grad.astype(jnp.bfloat16), 'dp', scatter_dimension=...  71.7 us
    reduce_scatter x1, waiting for transfers between devices, local(): lax.psum_scatter(normed_grad.astype(jnp.bfloat16), 'branch', scatter_dime...  71.5 us
    dot_general x3, matrix products, contract_rows(): lax.dot_general(left, right, (((0,), (0,)), ((), ())), preferred_element_...  39.7 us
    dot_general x3, matrix products, contract_cols(): lax.dot_general(left, right, (((1,), (1,)), ((), ())), preferred_element_...  37.7 us
    dot_general x4, matrix products, masked_scores(): jnp.einsum('hqd,hkd->hqk', query_blk, keys_rot, preferred_element_type=jn...  31.4 us
  transfers between devices with their start and end apart: 15, of which 8 were waited for; matrix products, arithmetic and copies ran while one was open for 39% of the time, Pallas kernels for 0%

profile of v1, /device:TPU:0, one launch (start us, length us, event | category | flops | bytes accessed | tf_op | source)
XLA Modules:
  0.0 848.1 jit_solution(3398362626419408266)
XLA Ops:
  11.7 42.1 %all-reduce.8 = (bf16[2048]{0:T(1024)(128)(2,1)S(1)}, bf16[2048]{0:T(1024)(128)(2,1)S(1)}, bf16[2048]{0:T(1024)(128)(2,1)}) all-reduce(bf16[2048]{0:T(1024)(128)(2,1)S(1)} %dynamic-update-slice.1, bf16[2048]{0:T(1024)(128)(2,1)S(1)} %dynamic-update-slice, ...), channel_id=1, replica_groups=mesh['dp'=8,'branch'=4] {'dp','branch'}, use_global_device_ids=true, to_apply=%add.1 | all-reduce | flops 6144 | bytes 24576
  69.1 46.6 %collective-permute-done = bf16[256,2048]{1,0:T(8,128)(2,1)S(1)} collective-permute-done((bf16[256,2048]{1,0:T(8,128)(2,1)S(1)}, bf16[256,2048]{1,0:T(8,128)(2,1)S(1)}, u32[]{:S(2)}, u32[]{:S(2)}) %collective-permute-start) | collective-permute-done | bytes 1048608 | tf_op jit(solution)/shard_map/ppermute | solution.py:177
  115.7 22.3 %collective-permute-start.1 = (bf16[256,2048]{1,0:T(8,128)(2,1)S(1)}, bf16[256,2048]{1,0:T(8,128)(2,1)S(1)}, u32[]{:S(2)}, u32[]{:S(2)}) collective-permute-start(bf16[256,2048]{1,0:T(8,128)(2,1)S(1)} %collective-permute-done), channel_id=1, source_target_pairs={{0,1},{1,2},{2,3},{3,0},{4,5},{5,6},{6,7},{7,4},{8,9},{9,10},{10,1... | collective-permute-start | bytes 3145736 | tf_op jit(solution)/shard_map/ppermute | solution.py:177
  140.8 40.7 %collective-permute-done.1 = bf16[256,2048]{1,0:T(8,128)(2,1)S(1)} collective-permute-done((bf16[256,2048]{1,0:T(8,128)(2,1)S(1)}, bf16[256,2048]{1,0:T(8,128)(2,1)S(1)}, u32[]{:S(2)}, u32[]{:S(2)}) %collective-permute-start.1) | collective-permute-done | bytes 1048608 | tf_op jit(solution)/shard_map/ppermute | solution.py:177
  183.9 7.9 all_gather.34
  192.5 9.6 %all_gather.37 = bf16[16,128]{0,1:T(8,128)(2,1)S(1)} all-gather(bf16[16,16]{0,1:T(8,128)(2,1)S(1)} %copy.79), channel_id=1, replica_groups=mesh['dp'=8,'branch'=4] {'dp'}, dimensions={1}, use_global_device_ids=true | all-gather | bytes 4608 | tf_op jit(solution)/shard_map/all_gather | solution.py:126
  203.3 3.1 collective-permute-done.2
  217.6 5.2 fusion.75
  225.9 5.4 all-gather.8.cloned.1.call-done
  231.4 10.1 %broadcast_add_fusion = f32[1024,3,512]{0,2,1:T(8,128)S(1)} fusion(f32[3,512]{1,0:T(4,128)S(1)} %reshape.336, bf16[3,2048,512]{1,2,0:T(8,128)(2,1)} %all-gather.8.cloned.1.call-done, bf16[1024,2048]{1,0:T(8,128)(2,1)} %all-gather.6.cloned.1.call-done), kind=kOutput, calls=%fused_computation.73 | convolution fusion | flops 6444023808 | bytes 16783360 | tf_op jit(solution)/shard_map/td,cde->cte/dot_general | solution.py:131
  244.9 31.3 %while.28 = (s32[]{:T(128)}, bf16[2,8,512,64]{2,3,1,0:T(8,128)(2,1)S(1)}, f32[2,8,512]{2,1,0:T(8,128)}, s32[2,512]{1,0:T(2,128)S(1)}, s32[1024]{0:T(1024)S(1)}, ...) while((s32[]{:T(128)}, ...), condition=%wide.region_7.8_spmd.clone, body=%wide.region_4.7_spmd.clone.sunk | while | flops 1125904384 | bytes 55723116 | solution.py:160
  245.5 4.1 fusion.134
  249.7 4.2 fusion.135
  254.5 5.9 fusion.136
  261.0 4.3 fusion.134
  265.3 4.2 fusion.135
  270.2 5.9 fusion.136
  278.6 97.0 %while.29 = (s32[]{:T(128)}, f32[8,1024,64]{1,2,0:T(8,128)}, f32[8,1024,64]{1,2,0:T(8,128)}, f32[2,8,512,64]{2,3,1,0:T(8,128)}, s32[2,512]{1,0:T(2,128)S(1)}, /*...) while((s32[]{:T(128)}, f32[8,1024,64]{1,2,0:T(8,128)}, ...), condition=%wide.region_11.12_spmd.clone, body=%wide.region_9.11_spmd.clone.sunk | while | flops 2726555648 | bytes 229738784 | solution.py:225
  280.0 3.8 fusion.146
  285.1 11.5 %multiply_reduce_fusion.2 = (f32[8,512]{1,0:T(8,128)}, f32[8,512,1024]{2,1,0:T(8,128)}) fusion(f32[8,512,1024]{2,1,0:T(8,128)S(1)} %fusion.146, f32[8,512]{1,0:T(8,128)} %dynamic-slice_bitcast_fusion.2, bf16[8,1024,64]{1,2,0:T(8,128)(2,1)S(1)} %get-tuple-element.598, bf16[2,8,512,64]{2,3,1,0:T(8,128)(2,1)} %get-tuple-element.597, ...), kind=kOutput, calls=%fused_computation.23.clone.1 | convolution fusion | flops 557838336 | bytes 35684864 | tf_op jit(solution)/shard_map/while/body/eval_jaxpr/hqd,hkd->hqk/dot_general | solution.py:77
  296.5 9.9 %multiply_convert_fusion.5 = bf16[8,512,1024]{2,1,0:T(8,128)(2,1)} fusion(f32[8,512,1024]{2,1,0:T(8,128)} %get-tuple-element.530, f32[8,512,1024]{2,1,0:T(8,128)S(1)} %fusion.146, f32[8,512]{1,0:T(8,128)} %get-tuple-element.531), kind=kLoop, calls=%fused_computation.22.clone.1 | loop fusion | flops 12582912 | bytes 41959424 | tf_op jit(solution)/shard_map/while/body/eval_jaxpr/convert_element_type | solution.py:212
  306.4 7.2 fusion.148
  313.7 5.5 select_add_fusion.4
  319.2 4.8 copy-done
  328.5 3.8 fusion.146
  333.6 11.5 %multiply_reduce_fusion.2 = (f32[8,512]{1,0:T(8,128)}, f32[8,512,1024]{2,1,0:T(8,128)}) fusion(f32[8,512,1024]{2,1,0:T(8,128)S(1)} %fusion.146, f32[8,512]{1,0:T(8,128)} %dynamic-slice_bitcast_fusion.2, bf16[8,1024,64]{1,2,0:T(8,128)(2,1)S(1)} %get-tuple-element.598, bf16[2,8,512,64]{2,3,1,0:T(8,128)(2,1)} %get-tuple-element.597, ...), kind=kOutput, calls=%fused_computation.23.clone.1 | convolution fusion | flops 557838336 | bytes 35684864 | tf_op jit(solution)/shard_map/while/body/eval_jaxpr/hqd,hkd->hqk/dot_general | solution.py:77
  345.1 9.3 %multiply_convert_fusion.5 = bf16[8,512,1024]{2,1,0:T(8,128)(2,1)} fusion(f32[8,512,1024]{2,1,0:T(8,128)} %get-tuple-element.530, f32[8,512,1024]{2,1,0:T(8,128)S(1)} %fusion.146, f32[8,512]{1,0:T(8,128)} %get-tuple-element.531), kind=kLoop, calls=%fused_computation.22.clone.1 | loop fusion | flops 12582912 | bytes 41959424 | tf_op jit(solution)/shard_map/while/body/eval_jaxpr/convert_element_type | solution.py:212
  354.4 7.2 fusion.148
  361.6 5.5 select_add_fusion.4
  367.1 3.6 copy-done
  370.9 4.5 select_add_fusion.5
  379.3 5.9 convolution_convert_fusion.2
  387.9 14.5 %fusion.88 = f32[1024,2048]{1,0:T(8,128)} fusion(bf16[1024,2048]{1,0:T(8,128)(2,1)} %all-gather.6.cloned.1.call-done, bf16[2048,2048]{1,0:T(8,128)(2,1)} %all-gather.12.cloned.1.call-done), kind=kOutput, calls=%fused_computation.158 | convolution fusion | flops 8589934592 | bytes 20971520 | tf_op jit(solution)/shard_map/dot_general | solution.py:162
  402.4 19.9 %fusion.87 = (bf16[2048]{0:T(1024)(128)(2,1)S(1)}, bf16[1024,2048]{1,0:T(8,128)(2,1)}) fusion(f32[1024,2048]{1,0:T(8,128)} %fusion.88, f32[2048]{0:T(1024)S(1)} %copy-done.28, bf16[2048,2048]{1,0:T(8,128)(2,1)} %all-gather.14.cloned.1.call-done, bf16[2048,2048]{1,0:T(8,128)(2,1)} %constant_dynamic-update-slice_fusion, s32[]{:T(128)S(6)} %select_n.31), kind=kOutput, calls=%fused_computation.157 | convolution fusion | flops 8636069888 | bytes 25178116 | tf_op jit(solution)/shard_map/dot_general | solution.py:70
  423.1 11.1 %convert_bitcast_fusion = bf16[3,2048,512]{1,2,0:T(8,128)(2,1)} fusion(bf16[3,1024,512]{1,2,0:T(8,128)(2,1)S(1)} %bitcast.175, bf16[1024,2048]{1,0:T(8,128)(2,1)} %all-gather.6.cloned.1.call-done), kind=kOutput, calls=%fused_computation.66 | convolution fusion | flops 6445596672 | bytes 13631488 | tf_op jit(solution)/shard_map/td,cte->cde/dot_general | solution.py:235
  434.4 12.6 %fusion.89 = f32[1024,2048]{1,0:T(8,128)S(1)} fusion(bf16[1024,2048]{1,0:T(8,128)(2,1)} %get-tuple-element.385, bf16[2048,2048]{1,0:T(8,128)(2,1)} %all-gather.12.cloned.1.call-done), kind=kOutput, calls=%fused_computation.159 | convolution fusion | flops 8589934592 | bytes 20971520 | tf_op jit(solution)/shard_map/dot_general | solution.py:70
  446.9 11.2 %fusion.44 = bf16[1024,2048]{1,0:T(8,128)(2,1)} fusion(f32[1024,2048]{1,0:T(8,128)S(1)} %fusion.89, bf16[3,1024,512]{1,2,0:T(8,128)(2,1)S(1)} %bitcast.176, bf16[3,2048,512]{1,2,0:T(8,128)(2,1)} %all-gather.8.cloned.1.call-done), kind=kOutput, calls=%fused_computation.60 | convolution fusion | flops 6446645248 | bytes 22020096 | tf_op jit(solution)/shard_map/cte,cde->td/dot_general | solution.py:237
  458.3 15.8 %fusion.84 = f32[1024,2048]{1,0:T(8,128)S(1)} fusion(bf16[2048,2048]{1,0:T(8,128)(2,1)} %all-gather.14.cloned.1.call-done, f32[1024,2048]{1,0:T(8,128)} %fusion.88, f32[2048]{0:T(1024)S(1)} %copy-done.28), kind=kOutput, calls=%fused_computation.155 | convolution fusion | flops 8610906112 | bytes 25174016 | tf_op jit(solution)/shard_map/dot_general | solution.py:167
  474.1 4.4 add_convert_fusion
  478.6 19.8 %convolution_convert_fusion = bf16[2048,2048]{1,0:T(8,128)(2,1)} fusion(bf16[2048,2048]{1,0:T(8,128)(2,1)} %constant_dynamic-update-slice_fusion, s32[]{:T(128)S(6)} %select_n.31, f32[1024,2048]{1,0:T(8,128)} %fusion.88, f32[2048]{0:T(1024)S(1)} %copy-done.28), kind=kOutput, calls=%fused_computation.63 | convolution fusion | flops 8615100416 | bytes 20979716 | tf_op jit(solution)/shard_map/dot_general | solution.py:64
  498.5 14.0 %convolution_convert_fusion.1 = bf16[2048,2048]{1,0:T(8,128)(2,1)} fusion(bf16[1024,2048]{1,0:T(8,128)(2,1)} %all-gather.6.cloned.1.call-done, bf16[1024,2048]{1,0:T(8,128)(2,1)} %get-tuple-element.385), kind=kOutput, calls=%fused_computation.64 | convolution fusion | flops 8594128896 | bytes 16777216 | tf_op jit(solution)/shard_map/dot_general | solution.py:64
  514.5 15.0 %all-reduce.6 = bf16[3,8,64]{2,1,0:T(8,128)(2,1)S(1)} all-reduce(bf16[3,8,64]{2,1,0:T(8,128)(2,1)S(1)} %copy-done.21), channel_id=8, replica_groups=mesh['dp'=8,'branch'=4] {'dp'}, use_global_device_ids=true, to_apply=%region_23.24.clone | all-reduce | flops 1536 | bytes 6144
  535.9 71.5 %reduce-scatter.13.cloned.1.call-done = bf16[256,2048]{1,0:T(8,128)(2,1)} async-done(((bf16[1024,2048]{1,0:T(8,128)(2,1)}), bf16[256,2048]{1,0:T(8,128)(2,1)}) %reduce-scatter.13.cloned.1.call-update) | async-done | bytes 1048592 | tf_op jit(solution)/shard_map/reduce_scatter | solution.py:260
  609.7 46.1 %all-reduce.7 = (f32[2048]{0:T(1024)S(1)}, f32[2048]{0:T(1024)S(1)}, f32[2048]{0:T(1024)S(1)}) all-reduce(f32[2048]{0:T(1024)S(1)} %get-tuple-element.302, f32[2048]{0:T(1024)S(1)} %get-tuple-element.305, f32[2048]{0:T(1024)S(1)} %copy-done.18), channel_id=4, replica_groups=mesh['dp'=8,'branch'=4] {'dp','branch'}, use_global_device_ids=true, to_apply=%region_16.17.clone | all-reduce | flops 6144 | bytes 49152
  657.5 30.4 %reduce-scatter.11.cloned.1.call-done = bf16[256,2048]{1,0:T(8,128)(2,1)} async-done(((bf16[1024,2048]{1,0:T(8,128)(2,1)}), bf16[256,2048]{1,0:T(8,128)(2,1)}) %reduce-scatter.11.cloned.1.call-update) | async-done | bytes 1048592 | tf_op jit(solution)/shard_map/reduce_scatter | solution.py:168
  687.9 4.0 fusion.71
  691.9 71.7 %reduce-scatter.21.cloned.1.call-done = bf16[2048,256]{1,0:T(8,128)(2,1)} async-done(((bf16[2048,2048]{1,0:T(8,128)(2,1)}), bf16[2048,256]{1,0:T(8,128)(2,1)}) %reduce-scatter.21.cloned.1.call-update) | async-done | bytes 1048592 | tf_op jit(solution)/shard_map/reduce_scatter | solution.py:256
  766.3 72.0 %reduce-scatter.19.cloned.1.call-done = bf16[256,2048]{1,0:T(8,128)(2,1)} async-done(((bf16[2048,2048]{1,0:T(8,128)(2,1)}), bf16[256,2048]{1,0:T(8,128)(2,1)}) %reduce-scatter.19.cloned.1.call-update) | async-done | bytes 1048592 | tf_op jit(solution)/shard_map/reduce_scatter | solution.py:250
  (206 shorter events, 82.3 us)
Async XLA Ops:
  7.2 210.4 %all-gather.10.cloned.1.call-start = ((), (), s32[]{:S(2)}) async-start(), calls=%async_computation.9 | async-start | bytes 2359296 | tf_op jit(solution)/shard_map/all_gather | solution.py:122
  9.0 216.9 %all-gather.6.cloned.1.call-start = ((), (), s32[]{:S(2)}) async-start(), calls=%async_computation.7 | async-start | bytes 5242880 | tf_op jit(solution)/shard_map/all_gather | solution.py:117
  53.8 3.2 copy-start.16
  53.8 12.8 %copy-start.6 = (bf16[256,2048]{1,0:T(8,128)(2,1)S(1)}, bf16[256,2048]{1,0:T(8,128)(2,1)}, u32[]{:S(2)}) copy-start(bf16[256,2048]{1,0:T(8,128)(2,1)} %param.20) | copy-start | bytes 3145732
  55.3 1.7 copy-start.19
  60.3 80.5 %copy-start.11 = (s32[1024]{0:T(1024)S(1)}, s32[1024]{0:T(1024)}, u32[]{:S(2)}) copy-start(s32[1024]{0:T(1024)} %param.18) | copy-start | bytes 12292
  60.3 123.5 %copy-start.24 = (f32[3,8,8]{2,1,0:T(8,128)S(1)}, f32[3,8,8]{2,1,0:T(8,128)}, u32[]{:S(2)}) copy-start(f32[3,8,8]{2,1,0:T(8,128)} %param.25) | copy-start | bytes 2308
  60.3 171.1 %all-gather.8.cloned.1.call-start = ((), (), s32[]{:S(2)}) async-start(), calls=%async_computation.8 | async-start | bytes 7077888 | tf_op jit(solution)/shard_map/all_gather | solution.py:120
  62.9 129.4 %copy-start.27 = (f32[16,16]{1,0:T(8,128)S(1)}, f32[16,16]{1,0:T(8,128)}, u32[]{:S(2)}) copy-start(f32[16,16]{1,0:T(8,128)} %param.28) | copy-start | bytes 3076
  63.0 325.0 %all-gather.12.cloned.1.call-start = ((), (), s32[]{:S(2)}) async-start(), calls=%async_computation.10 | async-start | bytes 9437184 | tf_op jit(solution)/shard_map/all_gather | solution.py:125
  65.7 336.7 %all-gather.14.cloned.1.call-start = ((), (), s32[]{:S(2)}) async-start(), calls=%async_computation.11 | async-start | bytes 9437184 | tf_op jit(solution)/shard_map/all_gather | solution.py:127
  66.6 117.2 %copy-start.25 = (f32[256]{0:T(256)}, f32[256]{0:T(256)S(1)}, u32[]{:S(2)}) copy-start(f32[256]{0:T(256)S(1)} %dynamic-slice_convert_fusion.1) | copy-start | bytes 3076
  67.5 48.2 %collective-permute-start = (bf16[256,2048]{1,0:T(8,128)(2,1)S(1)}, bf16[256,2048]{1,0:T(8,128)(2,1)S(1)}, u32[]{:S(2)}, u32[]{:S(2)}) collective-permute-start(bf16[256,2048]{1,0:T(8,128)(2,1)S(1)} %get-tuple-element.357), channel_id=1, source_target_pairs={{0,1},{1,2},{2,3},{3,0},{4,5},{5,6},{6,7},{7,4},{8,9},{9,10},{10,1... | collective-permute-start | bytes 3145736 | tf_op jit(solution)/shard_map/ppermute | solution.py:177
  115.7 65.8 %collective-permute-start.1 = (bf16[256,2048]{1,0:T(8,128)(2,1)S(1)}, bf16[256,2048]{1,0:T(8,128)(2,1)S(1)}, u32[]{:S(2)}, u32[]{:S(2)}) collective-permute-start(bf16[256,2048]{1,0:T(8,128)(2,1)S(1)} %collective-permute-done), channel_id=1, source_target_pairs={{0,1},{1,2},{2,3},{3,0},{4,5},{5,6},{6,7},{7,4},{8,9},{9,10},{10,1... | collective-permute-start | bytes 3145736 | tf_op jit(solution)/shard_map/ppermute | solution.py:177
  140.7 389.5 %reduce-scatter.17.cloned.1.call-start = ((), (), s32[]{:S(2)}) async-start(), calls=%async_computation.15 | async-start | bytes 2359296 | tf_op jit(solution)/shard_map/reduce_scatter | solution.py:247
  181.5 25.0 %collective-permute-start.2 = (bf16[256,2048]{1,0:T(8,128)(2,1)S(1)}, bf16[256,2048]{1,0:T(8,128)(2,1)}, u32[]{:S(2)}, u32[]{:S(2)}) collective-permute-start(bf16[256,2048]{1,0:T(8,128)(2,1)S(1)} %collective-permute-done.1), channel_id=1, source_target_pairs={{0,1},{1,2},{2,3},{3,0},{4,5},{5,6},{6,7},{7,4},{8,9},{9,10},{10,1... | collective-permute-start | bytes 3145736 | tf_op jit(solution)/shard_map/ppermute | solution.py:177
  203.3 40.1 %copy-start.12 = (f32[1024,16]{0,1:T(8,128)}, f32[1024,16]{0,1:T(8,128)S(1)}, u32[]{:S(2)}) copy-start(f32[1024,16]{0,1:T(8,128)S(1)} %get-tuple-element.382) | copy-start | bytes 196612
  203.3 40.1 %copy-start.14 = (f32[1024,16]{0,1:T(8,128)}, f32[1024,16]{0,1:T(8,128)S(1)}, u32[]{:S(2)}) copy-start(f32[1024,16]{0,1:T(8,128)S(1)} %get-tuple-element.383) | copy-start | bytes 196612
  243.2 1.7 copy-start.10
  306.4 7.2 copy-start.1
  313.7 10.3 %copy-start = (f32[8,512,1024]{2,1,0:T(8,128)S(1)}, f32[8,512,1024]{2,1,0:T(8,128)}, u32[]{:S(2)}) copy-start(f32[8,512,1024]{2,1,0:T(8,128)} %get-tuple-element.530) | copy-start | bytes 50331652 | tf_op jit(solution)/shard_map/while
  313.7 10.5 %copy-start.4 = (bf16[2,8,512,64]{2,3,1,0:T(8,128)(2,1)S(1)}, bf16[2,8,512,64]{2,3,1,0:T(8,128)(2,1)}, u32[]{:S(2)}) copy-start(bf16[2,8,512,64]{2,3,1,0:T(8,128)(2,1)} %get-tuple-element.600) | copy-start | bytes 3145732 | tf_op jit(solution)/shard_map/while
  319.1 8.0 copy-start.2
  354.4 7.2 copy-start.1
  361.6 9.1 %copy-start = (f32[8,512,1024]{2,1,0:T(8,128)S(1)}, f32[8,512,1024]{2,1,0:T(8,128)}, u32[]{:S(2)}) copy-start(f32[8,512,1024]{2,1,0:T(8,128)} %get-tuple-element.530) | copy-start | bytes 50331652 | tf_op jit(solution)/shard_map/while
  361.6 9.3 %copy-start.4 = (bf16[2,8,512,64]{2,3,1,0:T(8,128)(2,1)S(1)}, bf16[2,8,512,64]{2,3,1,0:T(8,128)(2,1)}, u32[]{:S(2)}) copy-start(bf16[2,8,512,64]{2,3,1,0:T(8,128)(2,1)} %get-tuple-element.600) | copy-start | bytes 3145732 | tf_op jit(solution)/shard_map/while
  367.1 8.3 copy-start.2
  375.6 3.4 copy-start.3
  375.6 3.4 copy-start.13
  375.6 3.4 copy-start.15
  375.6 3.7 copy-start.8
  385.2 146.7 %reduce-scatter.23.cloned.1.call-start = ((), (), s32[]{:S(2)}) async-start(), calls=%async_computation.18 | async-start | bytes 36864
  387.9 14.5 %copy-start.28 = (f32[2048]{0:T(1024)S(1)}, f32[2048]{0:T(1024)}, u32[]{:S(2)}) copy-start(f32[2048]{0:T(1024)} %bitcast_convert_fusion) | copy-start | bytes 24580
  423.1 110.2 %reduce-scatter.15.cloned.1.call-start = ((), (), s32[]{:S(2)}) async-start(), calls=%async_computation.14 | async-start | bytes 7077888 | tf_op jit(solution)/shard_map/reduce_scatter | solution.py:241
  434.3 173.1 %reduce-scatter.13.cloned.1.call-start = ((), (), s32[]{:S(2)}) async-start(), calls=%async_computation.13 | async-start | bytes 5242880 | tf_op jit(solution)/shard_map/reduce_scatter | solution.py:260
  458.2 15.9 %copy-start.9 = (bf16[64,8,2,512]{3,1,2,0:T(8,128)(2,1)S(1)}, bf16[64,8,2,512]{3,1,2,0:T(8,128)(2,1)}, u32[]{:S(2)}) copy-start(bf16[64,8,2,512]{3,1,2,0:T(8,128)(2,1)} %copy.97) | copy-start | bytes 3145732
  458.2 15.9 %copy-start.30 = (bf16[512,2048]{1,0:T(8,128)(2,1)S(1)}, bf16[512,2048]{1,0:T(8,128)(2,1)}, u32[]{:S(2)}) copy-start(bf16[512,2048]{1,0:T(8,128)(2,1)} %all-gather.10.cloned.1.call-done) | copy-start | bytes 6291460
  458.2 229.7 %reduce-scatter.11.cloned.1.call-start = ((), (), s32[]{:S(2)}) async-start(), calls=%async_computation.12 | async-start | bytes 5242880 | tf_op jit(solution)/shard_map/reduce_scatter | solution.py:168
  478.5 285.0 %reduce-scatter.21.cloned.1.call-start = ((), (), s32[]{:S(2)}) async-start(), calls=%async_computation.17 | async-start | bytes 9437184 | tf_op jit(solution)/shard_map/reduce_scatter | solution.py:256
  498.4 339.8 %reduce-scatter.19.cloned.1.call-start = ((), (), s32[]{:S(2)}) async-start(), calls=%async_computation.16 | async-start | bytes 9437184 | tf_op jit(solution)/shard_map/reduce_scatter | solution.py:250
  512.5 1.9 copy-start.21
  512.5 94.8 %copy-start.5 = (bf16[256,2048]{1,0:T(8,128)(2,1)S(1)}, bf16[256,2048]{1,0:T(8,128)(2,1)}, u32[]{:S(2)}) copy-start(bf16[256,2048]{1,0:T(8,128)(2,1)} %param.17) | copy-start | bytes 3145732
  512.5 94.8 %copy-start.17 = (f32[2048]{0:T(1024)S(1)}, f32[2048]{0:T(1024)}, u32[]{:S(2)}) copy-start(f32[2048]{0:T(1024)} %copy-done.16) | copy-start | bytes 24580
  512.6 94.8 %copy-start.20 = (f32[256]{0:T(256)S(1)}, f32[256]{0:T(256)}, u32[]{:S(2)}) copy-start(f32[256]{0:T(256)} %copy-done.19) | copy-start | bytes 3076
  512.6 94.8 %copy-start.23 = (f32[256]{0:T(256)S(1)}, f32[256]{0:T(256)}, u32[]{:S(2)}) copy-start(f32[256]{0:T(256)} %copy-done.22) | copy-start | bytes 3076
  512.6 97.1 %copy-start.18 = (f32[2048]{0:T(1024)S(1)}, f32[2048]{0:T(1024)}, u32[]{:S(2)}) copy-start(f32[2048]{0:T(1024)} %get-tuple-element.356) | copy-start | bytes 24580
  512.6 175.3 %copy-start.7 = (bf16[256,2048]{1,0:T(8,128)(2,1)S(1)}, bf16[256,2048]{1,0:T(8,128)(2,1)}, u32[]{:S(2)}) copy-start(bf16[256,2048]{1,0:T(8,128)(2,1)} %param.20) | copy-start | bytes 3145732
  512.6 175.3 %copy-start.26 = (f32[256]{0:T(256)S(1)}, f32[256]{0:T(256)}, u32[]{:S(2)}) copy-start(f32[256]{0:T(256)} %copy-done.25) | copy-start | bytes 3076
  (3 other events, 1.9 us)
Sparse Core Ops, SparseCore 0:
  10.5 30.9 all-gather.9
  60.4 123.8 all-gather.5
  186.2 45.1 all-gather.7
  233.7 54.3 all-gather.11
  290.4 55.9 all-gather.13
  385.3 41.9 reduce-scatter.16
  431.2 31.2 reduce-scatter.22
  465.9 62.1 reduce-scatter.14
  530.6 76.7 reduce-scatter.12
  609.5 78.3 reduce-scatter.10
  691.7 71.7 reduce-scatter.20
  766.9 71.2 reduce-scatter.18
